TPU v7x, 32 devices: a whole 2x2x4 slice. The times are simulated.
32 devices in a mesh: tm: 4 (over x, core), fibre: 8 (over z, y).
Axes of the slice: x: 2, y: 2, z: 4, core: 2. Of those that a mesh axis runs over, the one named last changes fastest.
Arguments:
- signal: float32 [64, 64, 1024], P(None, 'fibre', 'tm'), may hold values from -6 to 6
- first_kernel_weight: float32 [3, 3, 128, 64], replicated, may hold values from -0.25 to 0.25
- first_layer_bias: float32 [128], replicated, may hold values from -1 to 1
- first_residual_matrix: float32 [64, 64], replicated, may hold values from -0.75 to 0.75
- second_kernel_weight: float32 [3, 3, 128, 64], replicated, may hold values from -0.25 to 0.25
- second_layer_bias: float32 [128], replicated, may hold values from -1 to 1
- second_residual_matrix: float32 [64, 64], replicated, may hold values from -0.75 to 0.75
Outputs:
- features: float32 [64, 64, 1024], P(None, 'fibre', 'tm')
All inputs are finite; a program needn't handle non-finite values.
Results may differ from a plain program's by a relative error of at most 0.0001.
Values sent between devices are 32-bit elements; how exact they have to be, the bound alone decides.
A program may use at most 64 MiB of HBM per device.

v0:
```python
import jax
import jax.numpy as jnp
from jax import lax
from jax.sharding import PartitionSpec as P

DILATION_ONE = 128
DILATION_TWO = 256


def shifted(block, axis, distance):
    devices = range(lax.axis_size(axis))
    route = [(i - distance, i) for i in devices if i - distance in devices]
    return lax.ppermute(block, axis, route)


def with_halo(cells, sides, width):
    for axis, dim in sides:
        count = lax.axis_size(axis)
        ends = count - 1
        head = lax.slice_in_dim(cells, 0, width, axis=dim)
        tail = lax.slice_in_dim(cells, cells.shape[dim] - width, cells.shape[dim], axis=dim)
        cells = jnp.concatenate(
            [
                lax.ppermute(tail, axis, [(i, (i + 1) % count) for i in range(ends)]),
                cells,
                lax.ppermute(head, axis, [((i + 1) % count, i) for i in range(ends)]),
            ],
            axis=dim,
        )
    return cells


def apply_gated_layer(widened_input, weight, bias, mixing, dilation):
    fibre_out = widened_input.shape[1] - 2
    time_out = widened_input.shape[2] - 2 * dilation
    preact = jnp.zeros((weight.shape[2], fibre_out, time_out), jnp.float32) + bias[:, None, None]
    for across in range(3):
        for along in range(3):
            offset = 2 * dilation - along * dilation
            window = widened_input[:, across : across + fibre_out, offset : offset + time_out]
            preact = preact + jnp.einsum(
                "oc,cft->oft", weight[across, along], window, precision=lax.Precision.HIGHEST
            )
    channels = mixing.shape[0]
    gated = jnp.tanh(preact[:channels]) * jax.nn.sigmoid(preact[channels:])
    return widened_input[:, 1:-1, 2 * dilation :] + jnp.einsum(
        "oc,cft->oft", mixing, gated, precision=lax.Precision.HIGHEST
    )


def body(
    signal,
    first_kernel_weight,
    first_layer_bias,
    first_residual_matrix,
    second_kernel_weight,
    second_layer_bias,
    second_residual_matrix,
):
    block_length = signal.shape[2]
    second_reach_back = (2 * DILATION_TWO + block_length - 1) // block_length
    pieces = [signal]
    steps_back = 1
    pieces.insert(0, shifted(signal, "tm", steps_back))
    widened_input = jnp.concatenate(pieces, axis=2)
    widened_input = with_halo(widened_input, (("fibre", 1),), 1)
    between_layers = apply_gated_layer(
        widened_input, first_kernel_weight, first_layer_bias, first_residual_matrix, DILATION_ONE
    )
    pieces = [between_layers]
    for steps_back in range(1, second_reach_back + 1):
        pieces.insert(0, shifted(between_layers, "tm", steps_back))
    widened_input = jnp.concatenate(pieces, axis=2)
    widened_input = with_halo(widened_input, (("fibre", 1),), 1)
    return apply_gated_layer(
        widened_input, second_kernel_weight, second_layer_bias, second_residual_matrix, DILATION_TWO
    )


def solution(mesh):
    placed = (P(None, "fibre", "tm"), P(), P(), P(), P(), P(), P())
    return jax.shard_map(
        body, mesh=mesh, in_specs=placed, out_specs=P(None, "fibre", "tm"), check_vma=False
    )
```

profile of v0, /device:TPU:0, one launch (start us, length us, event | category | flops | bytes accessed | tf_op | source)
XLA Modules:
  0.0 69.3 jit_solution(14621484572439502241)
XLA Ops:
  0.0 0.0 copy-start
  0.0 1.3 %copy.11 = f32[64,8,256]{2,0,1:T(8,128)S(1)} copy(f32[64,8,256]{2,1,0:T(8,128)} %param.7) | data formatting | bytes 1048576 | tf_op args[0]
  1.3 2.4 %collective-permute-start = (f32[64,8,256]{2,0,1:T(8,128)S(1)}, f32[64,8,256]{2,0,1:T(8,128)S(1)}, u32[]{:S(2)}, u32[]{:S(2)}) collective-permute-start(f32[64,8,256]{2,0,1:T(8,128)S(1)} %copy.11), channel_id=1, source_target_pairs={{0,8},{8,16},{16,24},{1,9},{9,17},{17,25},{2,10},{10,18},{18,26},{... | collective-permute-start | bytes 1572872 | tf_op jit(solution)/shard_map/ppermute | solution.py:13
  3.7 0.0 copy-done.1
  3.7 0.0 copy-done.2
  3.8 1.1 %fusion.96 = f32[128,8,256]{2,0,1:T(8,128)S(1)} fusion(f32[3,3,128,64]{2,3,1,0:T(8,128)S(1)} %copy-done.2, f32[64,8,256]{2,1,0:T(8,128)S(1)} %copy-done.1), kind=kOutput, calls=%fused_computation.122 | convolution fusion | flops 201326592 | bytes 1605632 | tf_op jit(solution)/shard_map/oc,cft->oft/dot_general | solution.py:41
  4.8 0.4 collective-permute-done
  5.2 0.1 constant_dynamic-update-slice_fusion.1
  5.3 0.2 constant_dynamic-update-slice_fusion
  5.5 4.2 %collective-permute-start.1 = (f32[64,1,512]{2,0,1:T(8,128)S(1)}, f32[64,1,512]{2,0,1:T(8,128)S(1)}, u32[]{:S(2)}, u32[]{:S(2)}) collective-permute-start(f32[64,1,512]{2,0,1:T(8,128)S(1)} %get-tuple-element.7), channel_id=1, source_target_pairs={{0,1},{1,2},{2,3},{3,4},{4,5},{5,6},{6,7},{8,9},{9,10},{10,11},{11... | collective-permute-start | bytes 393224 | tf_op jit(solution)/shard_map/ppermute | solution.py:24
  9.7 1.3 %collective-permute-start.2 = (f32[64,1,512]{2,0,1:T(8,128)S(1)}, f32[64,1,512]{2,0,1:T(8,128)S(1)}, u32[]{:S(2)}, u32[]{:S(2)}) collective-permute-start(f32[64,1,512]{2,0,1:T(8,128)S(1)} %get-tuple-element.8), channel_id=1, source_target_pairs={{1,0},{2,1},{3,2},{4,3},{5,4},{6,5},{7,6},{9,8},{10,9},{11,10},{12... | collective-permute-start | bytes 393224 | tf_op jit(solution)/shard_map/ppermute | solution.py:26
  11.0 1.0 %fusion.93 = f32[128,8,256]{2,0,1:T(8,128)S(1)} fusion(f32[64,8,256]{2,0,1:T(8,128)S(1)} %collective-permute-done, f32[3,3,128,64]{2,3,1,0:T(8,128)S(1)} %copy-done.2), kind=kOutput, calls=%fused_computation.119 | convolution fusion | flops 201326592 | bytes 1605632 | tf_op jit(solution)/shard_map/oc,cft->oft/dot_general | solution.py:41
  12.1 0.2 collective-permute-done.1
  12.2 1.0 %fusion.24 = f32[8,256,128]{1,2,0:T(8,128)S(1)} fusion(f32[64,8,512]{2,0,1:T(8,128)S(1)} %constant_dynamic-update-slice_fusion, f32[64,1,512]{2,0,1:T(8,128)S(1)} %collective-permute-done.1, f32[3,3,128,64]{2,3,1,0:T(8,128)S(1)} %copy-done.2), kind=kOutput, calls=%fused_computation.39 | convolution fusion | flops 201457664 | bytes 2260992 | tf_op jit(solution)/shard_map/oc,cft->oft/dot_general | solution.py:41
  13.3 1.0 %fusion.75 = f32[8,256,128]{1,2,0:T(8,128)S(1)} fusion(f32[64,8,512]{2,0,1:T(8,128)S(1)} %constant_dynamic-update-slice_fusion, f32[64,1,512]{2,0,1:T(8,128)S(1)} %collective-permute-done.1, f32[3,3,128,64]{2,3,1,0:T(8,128)S(1)} %copy-done.2), kind=kOutput, calls=%fused_computation.98 | convolution fusion | flops 201457664 | bytes 2260992 | tf_op jit(solution)/shard_map/oc,cft->oft/dot_general | solution.py:41
  14.3 2.3 %collective-permute-done.2 = f32[64,1,512]{2,0,1:T(8,128)S(1)} collective-permute-done((f32[64,1,512]{2,0,1:T(8,128)S(1)}, f32[64,1,512]{2,0,1:T(8,128)S(1)}, u32[]{:S(2)}, u32[]{:S(2)}) %collective-permute-start.2) | collective-permute-done | bytes 131104 | tf_op jit(solution)/shard_map/ppermute | solution.py:26
  16.6 1.0 %convolution_bitcast_fusion.2 = f32[128,8,256]{2,0,1:T(8,128)S(1)} fusion(f32[64,8,512]{2,0,1:T(8,128)S(1)} %constant_dynamic-update-slice_fusion, f32[64,1,512]{2,0,1:T(8,128)S(1)} %collective-permute-done.2, f32[3,3,128,64]{2,3,1,0:T(8,128)S(1)} %copy-done.2), kind=kOutput, calls=%fused_computation.6 | convolution fusion | flops 201457664 | bytes 2260992 | tf_op jit(solution)/shard_map/oc,cft->oft/dot_general | solution.py:41
  17.6 1.0 %convolution_bitcast_fusion.1 = f32[128,8,256]{2,0,1:T(8,128)S(1)} fusion(f32[64,8,512]{2,0,1:T(8,128)S(1)} %constant_dynamic-update-slice_fusion, f32[64,1,512]{2,0,1:T(8,128)S(1)} %collective-permute-done.2, f32[3,3,128,64]{2,3,1,0:T(8,128)S(1)} %copy-done.2), kind=kOutput, calls=%fused_computation.5 | convolution fusion | flops 201457664 | bytes 2260992 | tf_op jit(solution)/shard_map/oc,cft->oft/dot_general | solution.py:41
  18.7 0.0 copy-start.4
  18.7 1.0 %convolution_bitcast_fusion = f32[128,8,256]{2,0,1:T(8,128)S(1)} fusion(f32[64,1,512]{2,0,1:T(8,128)S(1)} %collective-permute-done.2, f32[64,8,512]{2,0,1:T(8,128)S(1)} %constant_dynamic-update-slice_fusion, f32[3,3,128,64]{2,3,1,0:T(8,128)S(1)} %copy-done.2), kind=kOutput, calls=%fused_computation.4 | convolution fusion | flops 201457664 | bytes 2260992 | tf_op jit(solution)/shard_map/oc,cft->oft/dot_general | solution.py:41
  19.7 0.0 copy-done.4
  19.7 1.2 %fusion.16 = f32[128,8,256]{2,0,1:T(8,128)S(1)} fusion(f32[128,8,256]{2,0,1:T(8,128)S(1)} %fusion.96, f32[8,256,128]{1,2,0:T(8,128)S(1)} %fusion.75, f32[8,256,128]{1,2,0:T(8,128)S(1)} %fusion.24, f32[64,8,512]{2,0,1:T(8,128)S(1)} %constant_dynamic-update-slice_fusion, f32[64,1,512]{2,0,1:T(8,128)S(1)} %collective-permute-done.1, f32[128]{0:T(128)S(1)} %copy-done.4, ...), kind=kOutput, calls=%fused_computation.27 | convolution fusion | flops 202506240 | bytes 5407232 | tf_op jit(solution)/shard_map/oc,cft->oft/dot_general | solution.py:41
  20.9 1.3 %fusion.4 = f32[128,8,256]{2,0,1:T(8,128)S(1)} fusion(f32[128,8,256]{2,0,1:T(8,128)S(1)} %convolution_bitcast_fusion, f32[128,8,256]{2,0,1:T(8,128)S(1)} %convolution_bitcast_fusion.1, f32[128,8,256]{2,0,1:T(8,128)S(1)} %convolution_bitcast_fusion.2, f32[128,8,256]{2,0,1:T(8,128)S(1)} %fusion.93, f32[128,8,256]{2,0,1:T(8,128)S(1)} %fusion.16, ...), kind=kOutput, calls=%fused_computation.12 | convolution fusion | flops 202637312 | bytes 6848512 | tf_op jit(solution)/shard_map/oc,cft->oft/dot_general | solution.py:41
  22.3 0.0 copy-done
  22.3 0.0 copy-start.3
  22.3 0.9 %fusion.17 = f32[64,8,256]{2,0,1:T(8,128)S(1)} fusion(f32[128,8,256]{2,0,1:T(8,128)S(1)} %fusion.4, f32[64,64]{1,0:T(8,128)S(1)} %copy-done, f32[64,8,256]{2,1,0:T(8,128)S(1)} %copy-done.1), kind=kOutput, calls=%fused_computation.30 | convolution fusion | flops 101318656 | bytes 2113536 | tf_op jit(solution)/shard_map/oc,cft->oft/dot_general | solution.py:46
  23.2 10.7 %collective-permute-start.3 = (f32[64,8,256]{2,0,1:T(8,128)S(1)}, f32[64,8,256]{2,0,1:T(8,128)S(1)}, u32[]{:S(2)}, u32[]{:S(2)}) collective-permute-start(f32[64,8,256]{2,0,1:T(8,128)S(1)} %fusion.17), channel_id=1, source_target_pairs={{0,16},{8,24},{1,17},{9,25},{2,18},{10,26},{3,19},{11,27},{4,20},{... | collective-permute-start | bytes 1572872 | tf_op jit(solution)/shard_map/ppermute | solution.py:13
  33.8 1.3 %collective-permute-start.4 = (f32[64,8,256]{2,0,1:T(8,128)S(1)}, f32[64,8,256]{2,0,1:T(8,128)S(1)}, u32[]{:S(2)}, u32[]{:S(2)}) collective-permute-start(f32[64,8,256]{2,0,1:T(8,128)S(1)} %fusion.17), channel_id=1, source_target_pairs={{0,8},{8,16},{16,24},{1,9},{9,17},{17,25},{2,10},{10,18},{18,26},{... | collective-permute-start | bytes 1572872 | tf_op jit(solution)/shard_map/ppermute | solution.py:13
  35.2 0.0 copy-done.3
  35.2 1.0 %fusion.85 = f32[8,256,128]{1,2,0:T(8,128)S(1)} fusion(f32[64,8,256]{2,0,1:T(8,128)S(1)} %fusion.17, f32[3,3,128,64]{2,3,1,0:T(8,128)S(1)} %copy-done.3), kind=kOutput, calls=%fused_computation.111 | convolution fusion | flops 201326592 | bytes 1605632 | tf_op jit(solution)/shard_map/oc,cft->oft/dot_general | solution.py:41
  36.2 9.9 %collective-permute-done.3 = f32[64,8,256]{2,0,1:T(8,128)S(1)} collective-permute-done((f32[64,8,256]{2,0,1:T(8,128)S(1)}, f32[64,8,256]{2,0,1:T(8,128)S(1)}, u32[]{:S(2)}, u32[]{:S(2)}) %collective-permute-start.3) | collective-permute-done | bytes 524320 | tf_op jit(solution)/shard_map/ppermute | solution.py:13
  46.1 0.0 collective-permute-done.4
  46.1 4.3 %collective-permute-start.5 = (f32[64,1,768]{2,0,1:T(8,128)S(1)}, f32[64,1,768]{2,0,1:T(8,128)S(1)}, u32[]{:S(2)}, u32[]{:S(2)}) collective-permute-start(f32[64,1,768]{2,0,1:T(8,128)S(1)} %get-tuple-element.5), channel_id=1, source_target_pairs={{0,1},{1,2},{2,3},{3,4},{4,5},{5,6},{6,7},{8,9},{9,10},{10,11},{11... | collective-permute-start | bytes 589832 | tf_op jit(solution)/shard_map/ppermute | solution.py:24
  50.5 1.5 %collective-permute-start.6 = (f32[64,1,768]{2,0,1:T(8,128)S(1)}, f32[64,1,768]{2,0,1:T(8,128)S(1)}, u32[]{:S(2)}, u32[]{:S(2)}) collective-permute-start(f32[64,1,768]{2,0,1:T(8,128)S(1)} %get-tuple-element.6), channel_id=1, source_target_pairs={{1,0},{2,1},{3,2},{4,3},{5,4},{6,5},{7,6},{9,8},{10,9},{11,10},{12... | collective-permute-start | bytes 589832 | tf_op jit(solution)/shard_map/ppermute | solution.py:26
  52.0 1.0 %fusion.82 = f32[8,256,128]{1,2,0:T(8,128)S(1)} fusion(f32[64,8,256]{2,0,1:T(8,128)S(1)} %collective-permute-done.3, f32[3,3,128,64]{2,3,1,0:T(8,128)S(1)} %copy-done.3), kind=kOutput, calls=%fused_computation.108 | convolution fusion | flops 201326592 | bytes 1605632 | tf_op jit(solution)/shard_map/oc,cft->oft/dot_general | solution.py:41
  53.0 6.7 %collective-permute-done.5 = f32[64,1,768]{2,0,1:T(8,128)S(1)} collective-permute-done((f32[64,1,768]{2,0,1:T(8,128)S(1)}, f32[64,1,768]{2,0,1:T(8,128)S(1)}, u32[]{:S(2)}, u32[]{:S(2)}) %collective-permute-start.5) | collective-permute-done | bytes 196640 | tf_op jit(solution)/shard_map/ppermute | solution.py:24
  59.6 1.0 %fusion.53 = f32[8,256,128]{1,2,0:T(8,128)S(1)} fusion(f32[64,1,768]{2,0,1:T(8,128)S(1)} %collective-permute-done.5, f32[64,8,256]{2,0,1:T(8,128)S(1)} %fusion.17, f32[64,8,256]{2,0,1:T(8,128)S(1)} %collective-permute-done.4, f32[64,8,256]{2,0,1:T(8,128)S(1)} %collective-permute-done.3, f32[3,3,128,64]{2,3,1,0:T(8,128)S(1)} %copy-done.3), kind=kOutput, calls=%fused_computation.73 | convolution fusion | flops 201719808 | bytes 2850816 | tf_op jit(solution)/shard_map/oc,cft->oft/dot_general | solution.py:41
  60.7 1.0 %fusion.51 = f32[8,256,128]{1,2,0:T(8,128)S(1)} fusion(f32[64,1,768]{2,0,1:T(8,128)S(1)} %collective-permute-done.5, f32[64,8,256]{2,0,1:T(8,128)S(1)} %fusion.17, f32[64,8,256]{2,0,1:T(8,128)S(1)} %collective-permute-done.4, f32[64,8,256]{2,0,1:T(8,128)S(1)} %collective-permute-done.3, f32[3,3,128,64]{2,3,1,0:T(8,128)S(1)} %copy-done.3), kind=kOutput, calls=%fused_computation.69 | convolution fusion | flops 201719808 | bytes 2850816 | tf_op jit(solution)/shard_map/oc,cft->oft/dot_general | solution.py:41
  61.7 0.0 collective-permute-done.6
  61.7 1.0 %fusion.43 = f32[8,256,128]{1,2,0:T(8,128)S(1)} fusion(f32[64,1,768]{2,0,1:T(8,128)S(1)} %collective-permute-done.6, f32[64,8,256]{2,0,1:T(8,128)S(1)} %fusion.17, f32[64,8,256]{2,0,1:T(8,128)S(1)} %collective-permute-done.4, f32[64,8,256]{2,0,1:T(8,128)S(1)} %collective-permute-done.3, f32[3,3,128,64]{2,3,1,0:T(8,128)S(1)} %copy-done.3), kind=kOutput, calls=%fused_computation.60 | convolution fusion | flops 201719808 | bytes 2850816 | tf_op jit(solution)/shard_map/oc,cft->oft/dot_general | solution.py:41
  62.7 1.0 %fusion.35 = f32[8,256,128]{1,2,0:T(8,128)S(1)} fusion(f32[64,1,768]{2,0,1:T(8,128)S(1)} %collective-permute-done.6, f32[64,8,256]{2,0,1:T(8,128)S(1)} %fusion.17, f32[64,8,256]{2,0,1:T(8,128)S(1)} %collective-permute-done.4, f32[64,8,256]{2,0,1:T(8,128)S(1)} %collective-permute-done.3, f32[3,3,128,64]{2,3,1,0:T(8,128)S(1)} %copy-done.3), kind=kOutput, calls=%fused_computation.52 | convolution fusion | flops 201719808 | bytes 2850816 | tf_op jit(solution)/shard_map/oc,cft->oft/dot_general | solution.py:41
  63.8 0.0 copy-start.5
  63.8 1.0 %fusion.33 = f32[8,256,128]{1,2,0:T(8,128)S(1)} fusion(f32[64,1,768]{2,0,1:T(8,128)S(1)} %collective-permute-done.6, f32[64,8,256]{2,0,1:T(8,128)S(1)} %fusion.17, f32[64,8,256]{2,0,1:T(8,128)S(1)} %collective-permute-done.4, f32[64,8,256]{2,0,1:T(8,128)S(1)} %collective-permute-done.3, f32[3,3,128,64]{2,3,1,0:T(8,128)S(1)} %copy-done.3), kind=kOutput, calls=%fused_computation.48 | convolution fusion | flops 201719808 | bytes 2850816 | tf_op jit(solution)/shard_map/oc,cft->oft/dot_general | solution.py:41
  64.8 1.2 %fusion.12 = f32[8,256,128]{1,2,0:T(8,128)S(1)} fusion(f32[8,256,128]{1,2,0:T(8,128)S(1)} %fusion.85, f32[8,256,128]{1,2,0:T(8,128)S(1)} %fusion.51, f32[8,256,128]{1,2,0:T(8,128)S(1)} %fusion.53, f32[64,1,768]{2,0,1:T(8,128)S(1)} %collective-permute-done.5, f32[64,8,256]{2,0,1:T(8,128)S(1)} %fusion.17, f32[64,8,256]{2,0,1:T(8,128)S(1)} %collective-permute-done.4, ...), kind=kOutput, calls=%fused_computation.22 | convolution fusion | flops 202768384 | bytes 5997056 | tf_op jit(solution)/shard_map/oc,cft->oft/dot_general | solution.py:41
  66.0 0.0 copy-start.6
  66.1 1.3 %fusion.9 = f32[128,8,256]{2,0,1:T(8,128)S(1)} fusion(f32[8,256,128]{1,2,0:T(8,128)S(1)} %fusion.33, f32[8,256,128]{1,2,0:T(8,128)S(1)} %fusion.35, f32[8,256,128]{1,2,0:T(8,128)S(1)} %fusion.43, f32[8,256,128]{1,2,0:T(8,128)S(1)} %fusion.82, f32[8,256,128]{1,2,0:T(8,128)S(1)} %fusion.12, f32[64,8,256]{2,0,1:T(8,128)S(1)} %collective-permute-done.4, ...), kind=kOutput, calls=%fused_computation.18 | convolution fusion | flops 202637312 | bytes 6848512 | tf_op jit(solution)/shard_map/oc,cft->oft/dot_general | solution.py:41
  67.4 0.8 %fusion.18 = f32[64,8,256]{2,0,1:T(8,128)S(1)} fusion(f32[64,8,256]{2,0,1:T(8,128)S(1)} %fusion.17, f32[128,8,256]{2,0,1:T(8,128)S(1)} %fusion.9, f32[64,64]{1,0:T(8,128)S(1)} %copy-done.6), kind=kOutput, calls=%fused_computation.31 | convolution fusion | flops 101318656 | bytes 2113536 | tf_op jit(solution)/shard_map/oc,cft->oft/dot_general | solution.py:46
  68.2 1.1 %copy.12 = f32[64,8,256]{2,1,0:T(8,128)} copy(f32[64,8,256]{2,0,1:T(8,128)S(1)} %fusion.18) | data formatting | bytes 1048576 | tf_op jit(solution)/shard_map/add | solution.py:46
  (6 shorter events, 0.1 us)
Async XLA Ops:
  0.0 22.3 %copy-start = (f32[64,64]{1,0:T(8,128)S(1)}, f32[64,64]{1,0:T(8,128)}, u32[]{:S(2)}) copy-start(f32[64,64]{1,0:T(8,128)} %param.10) | copy-start | bytes 49156
  0.0 3.7 %copy-start.1 = (f32[64,8,256]{2,1,0:T(8,128)S(1)}, f32[64,8,256]{2,1,0:T(8,128)}, u32[]{:S(2)}) copy-start(f32[64,8,256]{2,1,0:T(8,128)} %param.7) | copy-start | bytes 1572868
  0.0 3.7 %copy-start.2 = (f32[3,3,128,64]{2,3,1,0:T(8,128)S(1)}, f32[3,3,128,64]{2,3,1,0:T(8,128)}, u32[]{:S(2)}) copy-start(f32[3,3,128,64]{2,3,1,0:T(8,128)} %param.8) | copy-start | bytes 884740
  1.3 3.9 %collective-permute-start = (f32[64,8,256]{2,0,1:T(8,128)S(1)}, f32[64,8,256]{2,0,1:T(8,128)S(1)}, u32[]{:S(2)}, u32[]{:S(2)}) collective-permute-start(f32[64,8,256]{2,0,1:T(8,128)S(1)} %copy.11), channel_id=1, source_target_pairs={{0,8},{8,16},{16,24},{1,9},{9,17},{17,25},{2,10},{10,18},{18,26},{... | collective-permute-start | bytes 1572872 | tf_op jit(solution)/shard_map/ppermute | solution.py:13
  5.5 6.8 %collective-permute-start.1 = (f32[64,1,512]{2,0,1:T(8,128)S(1)}, f32[64,1,512]{2,0,1:T(8,128)S(1)}, u32[]{:S(2)}, u32[]{:S(2)}) collective-permute-start(f32[64,1,512]{2,0,1:T(8,128)S(1)} %get-tuple-element.7), channel_id=1, source_target_pairs={{0,1},{1,2},{2,3},{3,4},{4,5},{5,6},{6,7},{8,9},{9,10},{10,11},{11... | collective-permute-start | bytes 393224 | tf_op jit(solution)/shard_map/ppermute | solution.py:24
  9.7 6.9 %collective-permute-start.2 = (f32[64,1,512]{2,0,1:T(8,128)S(1)}, f32[64,1,512]{2,0,1:T(8,128)S(1)}, u32[]{:S(2)}, u32[]{:S(2)}) collective-permute-start(f32[64,1,512]{2,0,1:T(8,128)S(1)} %get-tuple-element.8), channel_id=1, source_target_pairs={{1,0},{2,1},{3,2},{4,3},{5,4},{6,5},{7,6},{9,8},{10,9},{11,10},{12... | collective-permute-start | bytes 393224 | tf_op jit(solution)/shard_map/ppermute | solution.py:26
  18.7 1.0 %copy-start.4 = (f32[128]{0:T(128)S(1)}, f32[128]{0:T(128)}, u32[]{:S(2)}) copy-start(f32[128]{0:T(128)} %param.9) | copy-start | bytes 1540
  22.3 12.9 %copy-start.3 = (f32[3,3,128,64]{2,3,1,0:T(8,128)S(1)}, f32[3,3,128,64]{2,3,1,0:T(8,128)}, u32[]{:S(2)}) copy-start(f32[3,3,128,64]{2,3,1,0:T(8,128)} %param.11) | copy-start | bytes 884740
  23.2 22.9 %collective-permute-start.3 = (f32[64,8,256]{2,0,1:T(8,128)S(1)}, f32[64,8,256]{2,0,1:T(8,128)S(1)}, u32[]{:S(2)}, u32[]{:S(2)}) collective-permute-start(f32[64,8,256]{2,0,1:T(8,128)S(1)} %fusion.17), channel_id=1, source_target_pairs={{0,16},{8,24},{1,17},{9,25},{2,18},{10,26},{3,19},{11,27},{4,20},{... | collective-permute-start | bytes 1572872 | tf_op jit(solution)/shard_map/ppermute | solution.py:13
  33.8 12.3 %collective-permute-start.4 = (f32[64,8,256]{2,0,1:T(8,128)S(1)}, f32[64,8,256]{2,0,1:T(8,128)S(1)}, u32[]{:S(2)}, u32[]{:S(2)}) collective-permute-start(f32[64,8,256]{2,0,1:T(8,128)S(1)} %fusion.17), channel_id=1, source_target_pairs={{0,8},{8,16},{16,24},{1,9},{9,17},{17,25},{2,10},{10,18},{18,26},{... | collective-permute-start | bytes 1572872 | tf_op jit(solution)/shard_map/ppermute | solution.py:13
  46.1 13.5 %collective-permute-start.5 = (f32[64,1,768]{2,0,1:T(8,128)S(1)}, f32[64,1,768]{2,0,1:T(8,128)S(1)}, u32[]{:S(2)}, u32[]{:S(2)}) collective-permute-start(f32[64,1,768]{2,0,1:T(8,128)S(1)} %get-tuple-element.5), channel_id=1, source_target_pairs={{0,1},{1,2},{2,3},{3,4},{4,5},{5,6},{6,7},{8,9},{9,10},{10,11},{11... | collective-permute-start | bytes 589832 | tf_op jit(solution)/shard_map/ppermute | solution.py:24
  50.5 11.2 %collective-permute-start.6 = (f32[64,1,768]{2,0,1:T(8,128)S(1)}, f32[64,1,768]{2,0,1:T(8,128)S(1)}, u32[]{:S(2)}, u32[]{:S(2)}) collective-permute-start(f32[64,1,768]{2,0,1:T(8,128)S(1)} %get-tuple-element.6), channel_id=1, source_target_pairs={{1,0},{2,1},{3,2},{4,3},{5,4},{6,5},{7,6},{9,8},{10,9},{11,10},{12... | collective-permute-start | bytes 589832 | tf_op jit(solution)/shard_map/ppermute | solution.py:26
  63.8 1.0 %copy-start.5 = (f32[128]{0:T(128)S(1)}, f32[128]{0:T(128)}, u32[]{:S(2)}) copy-start(f32[128]{0:T(128)} %param.12) | copy-start | bytes 1540
  66.0 1.4 %copy-start.6 = (f32[64,64]{1,0:T(8,128)S(1)}, f32[64,64]{1,0:T(8,128)}, u32[]{:S(2)}) copy-start(f32[64,64]{1,0:T(8,128)} %param.13) | copy-start | bytes 49156
where the time goes:
time: 69.6 us; the launch traced here: 69.3 us
  starting transfers between devices  25.8 us (37%)
  matrix products  21.1 us (30%)
  waiting for transfers between devices  19.4 us (28%)
  local copies, waits for them, and re-layouts  2.65 us (4%)
    dot_general x18, matrix products, apply_gated_layer(): jnp.einsum('oc,cft->oft', weight[across, along], window, precision=lax.Pr...  19.4 us
    ppermute x3, starting transfers between devices, shifted(): return lax.ppermute(block, axis, route)  14.4 us
    ppermute x3, waiting for transfers between devices, shifted(): return lax.ppermute(block, axis, route)  10.3 us
    ppermute x2, starting transfers between devices, with_halo(): lax.ppermute(tail, axis, [(i, (i + 1) % count) for i in range(ends)])  8.58 us
    ppermute x2, waiting for transfers between devices, with_halo(): lax.ppermute(tail, axis, [(i, (i + 1) % count) for i in range(ends)])  6.83 us
    ppermute x2, starting transfers between devices, with_halo(): lax.ppermute(head, axis, [((i + 1) % count, i) for i in range(ends)])  2.76 us
    ppermute x2, waiting for transfers between devices, with_halo(): lax.ppermute(head, axis, [((i + 1) % count, i) for i in range(ends)])  2.31 us
    dot_general x2, matrix products, apply_gated_layer(): jnp.einsum('oc,cft->oft', mixing, gated, precision=lax.Precision.HIGHEST)  1.64 us
  transfers between devices with their start and end apart: 7, of which 5 were waited for; matrix products, arithmetic and copies ran while one was open for 12% of the time, Pallas kernels for 0%

commit v1 on v0

v1 whole, which is shorter than its diff:
```python
import jax
import jax.numpy as jnp
from jax import lax
from jax.experimental import pallas as pl
from jax.experimental.pallas import tpu as pltpu
from jax.sharding import PartitionSpec as P

DILATION_ONE = 128
DILATION_TWO = 256
BF = jnp.bfloat16
F32 = jnp.float32


def split(value):
    hi = value.astype(BF)
    return hi, (value - hi.astype(F32)).astype(BF)


def thirds(value):
    hi, lo = split(value)
    return [hi, lo, hi]


def kernel(
    nt, nf, fib,
    x_hbm, w1_hbm, b1_hbm, r1_hbm, w2_hbm, b2_hbm, r2_hbm, out_ref,
    s, m, w1, b1, r1, w2, b2, r2, l1, l2, q1, q2, c1, c2, aa, bb,
    in_sem, w_sem, h0s, h0r, xs, xr, h2s, h2r, ps, pr, ts, tr, ms, mr, es, er,
):
    T = lax.axis_index("tm")
    F = lax.axis_index("fibre")
    odd = lax.rem(T, 2)
    even = odd == 0
    isodd = odd == 1
    partner = T + 1 - 2 * odd
    ch = x_hbm.shape[1]
    wide = fib + 4
    mid = fib + 2
    out_ch = 2 * ch
    far = nt > 4
    up, down = F + 1 < nf, F > 0

    def dev(t, f):
        return {"tm": t, "fibre": f}

    ins = [
        pltpu.make_async_copy(x_hbm.at[f], s.at[0, f + 2], in_sem.at[f]) for f in range(fib)
    ]
    for c in ins:
        c.start()
    weights = [
        pltpu.make_async_copy(a, b, w_sem.at[i])
        for i, (a, b) in enumerate(
            [(w1_hbm, w1), (b1_hbm, b1), (r1_hbm, r1), (w2_hbm, w2), (b2_hbm, b2), (r2_hbm, r2)]
        )
    ]
    for c in weights:
        c.start()

    barrier = pltpu.get_barrier_semaphore()
    friends = [(partner, F, None), (T, F + 1, up), (T, F - 1, down), (T + 2, F, T + 2 < nt), (T - 2, F, T >= 2)]
    if far:
        send3 = isodd & (T + 3 < nt)
        recv3 = even & (T >= 4)
        for e, ok in ((0, None), (1, up), (-1, down)):
            for d, okt in ((3, send3), (-3, recv3)):
                friends.append((T + d, F + e, okt if ok is None else okt & ok))
    count = jnp.int32(0)
    for t, f, ok in friends:
        if ok is None:
            pl.semaphore_signal(barrier, inc=1, device_id=dev(t, f), device_id_type=pl.DeviceIdType.MESH)
            count = count + 1
        else:
            @pl.when(ok)
            def _(t=t, f=f):
                pl.semaphore_signal(barrier, inc=1, device_id=dev(t, f), device_id_type=pl.DeviceIdType.MESH)
            count = count + ok.astype(jnp.int32)
    pl.semaphore_wait(barrier, count)

    def remote(src, dst, ssem, rsem, t, f):
        return pltpu.make_async_remote_copy(
            src_ref=src, dst_ref=dst, send_sem=ssem, recv_sem=rsem,
            device_id=dev(t, f), device_id_type=pl.DeviceIdType.MESH,
        )

    def halo_up(j, ss, rr):
        return remote(s.at[j, pl.ds(fib, 2)], s.at[j, pl.ds(0, 2)], ss.at[0], rr.at[0], T, F + 1)

    def halo_down(j, ss, rr):
        return remote(s.at[j, pl.ds(2, 2)], s.at[j, pl.ds(fib + 2, 2)], ss.at[1], rr.at[1], T, F - 1)

    def cross(f):
        return remote(x_hbm.at[f], s.at[2, f + 2], xs.at[f], xr.at[f], T + 2, F)

    order = [0, 1, fib - 2, fib - 1] + list(range(2, fib - 2))

    @pl.when(T + 2 < nt)
    def _():
        for f in order:
            cross(f).start()

    for f in (0, 1, fib - 2, fib - 1):
        ins[f].wait()

    @pl.when(up)
    def _():
        halo_up(0, h0s, h0r).start()

    @pl.when(down)
    def _():
        halo_down(0, h0s, h0r).start()

    if far:
        def third(i, e):
            if e == 0:
                src, dst = x_hbm, s.at[3, pl.ds(2, fib)]
            elif e == 1:
                src, dst = x_hbm.at[pl.ds(fib - 2, 2)], s.at[3, pl.ds(0, 2)]
            else:
                src, dst = x_hbm.at[pl.ds(0, 2)], s.at[3, pl.ds(fib + 2, 2)]
            return remote(src, dst, es.at[i], er.at[i], T + 3, F + e)

        thirds_list = [(0, 0, None, None), (1, 1, up, down), (2, -1, down, up)]
        for i, e, ok, _ok in thirds_list:
            @pl.when(send3 if ok is None else send3 & ok)
            def _(i=i, e=e):
                third(i, e).start()

    zero2 = jnp.zeros((2,) + s.shape[2:], F32)

    def zero_halo(j):
        @pl.when(jnp.logical_not(down))
        def _():
            s[j, pl.ds(0, 2)] = zero2

        @pl.when(jnp.logical_not(up))
        def _():
            s[j, pl.ds(fib + 2, 2)] = zero2

    zero_halo(0)

    @pl.when(T >= 2)
    def _():
        zero_halo(2)

    @pl.when(T == 0)
    def _():
        s[1] = jnp.zeros(s.shape[1:], F32)
        m[1] = jnp.zeros(m.shape[1:], F32)

    @pl.when(T < 2)
    def _():
        m[2] = jnp.zeros(m.shape[1:], F32)

    @pl.when(T == 2)
    def _():
        s[3] = jnp.zeros(s.shape[1:], F32)

    if far:
        @pl.when(recv3)
        def _():
            zero_halo(3)

    for f in range(2, fib - 2):
        ins[f].wait()
    for c in weights:
        c.wait()

    def prepare(w, left, r, mix, bias, tall):
        for a in range(3):
            for k in range(3):
                hi, lo = split(w[a, k])
                for i, piece in enumerate((hi, hi, lo)):
                    left[pl.ds(a * out_ch, out_ch), pl.ds((3 * k + i) * ch, ch)] = piece
        hi, lo = split(r[...])
        for i, piece in enumerate((hi, hi, lo)):
            mix[:, pl.ds(i * ch, ch)] = piece
        tall[...] = jnp.broadcast_to(bias[...], (out_ch, out_ch)).T

    prepare(w1, l1, r1, q1, b1, c1)
    prepare(w2, l2, r2, q2, b2, c2)

    def wait_halos(j, ss, rr):
        @pl.when(down)
        def _():
            halo_up(j, ss, rr).wait_recv()

        @pl.when(up)
        def _():
            halo_down(j, ss, rr).wait_recv()

    def push(slot, g, left, pieces):
        right = jnp.concatenate(pieces, axis=0)
        p = jnp.dot(left[...], right, preferred_element_type=F32)
        total = bb[slot] + p[2 * out_ch:]
        bb[slot] = aa[slot] + p[out_ch:2 * out_ch]
        aa[slot] = p[:out_ch]
        return total

    def gate(total, mix, tall, base):
        bias = tall[...]
        bias = jnp.concatenate([bias] * (total.shape[1] // bias.shape[1]), axis=1)
        pre = total + bias
        g = jnp.tanh(pre[:ch]) * (0.5 * jnp.tanh(0.5 * pre[ch:]) + 0.5)
        return base + jnp.dot(mix[...], jnp.concatenate(thirds(g), axis=0), preferred_element_type=F32)

    def first(slot, g, cur, prev, dst):
        chi, clo = split(s[cur, g])
        phi, plo = split(s[prev, g])
        d = DILATION_ONE
        shi = jnp.concatenate([phi[:, d:], chi[:, :d]], axis=1)
        slo = jnp.concatenate([plo[:, d:], clo[:, :d]], axis=1)
        total = push(slot, g, l1, [chi, clo, chi, shi, slo, shi, phi, plo, phi])

        @pl.when(g >= 2)
        def _():
            h = g - 2
            value = gate(total, q1, c1, s[cur, g - 1])
            row = F * fib + h - 1
            ok = (row >= 0) & (row < nf * fib)
            m[dst, h] = jnp.where(ok, value, 0.0)

    aa[...] = jnp.zeros_like(aa)
    bb[...] = jnp.zeros_like(bb)

    def part(src, g):
        return remote(s.at[src, g], s.at[1, g], ps.at[g], pr.at[g], partner, F)

    def part3(g):
        return remote(s.at[2, g], s.at[3, g], ts.at[g], tr.at[g], partner, F)

    def share(src, h):
        return remote(m.at[src, h], m.at[1, h], ms.at[h], mr.at[h], partner, F)

    wait_halos(0, h0s, h0r)

    @pl.when(even)
    def _():
        for g in range(wide):
            part(0, g).start()

    @pl.when(T >= 2)
    def _():
        for f in (0, 1, fib - 2, fib - 1):
            cross(f).wait_recv()

        @pl.when(up)
        def _():
            halo_up(2, h2s, h2r).start()

        @pl.when(down)
        def _():
            halo_down(2, h2s, h2r).start()

        wait_halos(2, h2s, h2r)

    if far:
        for i, e, _ok, ok in thirds_list:
            @pl.when(recv3 if ok is None else recv3 & ok)
            def _(i=i, e=e):
                third(i, e).wait_recv()

    def send_mid(h):
        @pl.when(even)
        def _():
            share(0, h).start()

        @pl.when(isodd & (T >= 2))
        def _():
            share(2, h).start()

    def step(g, carry):
        @pl.when(T >= 2)
        def _():
            @pl.when((g >= 4) & (g < fib))
            def _():
                cross(g - 2).wait_recv()

            @pl.when(even)
            def _():
                part3(g).start()

            @pl.when(isodd)
            def _():
                part(2, g).start()
                part3(g).wait_recv()

            first(1, g, 2, 3, 2)

        @pl.when(T >= 1)
        def _():
            part(0, g).wait_recv()

        first(0, g, 0, 1, 0)

        @pl.when(g >= 3)
        def _():
            send_mid(g - 3)
        return carry

    lax.fori_loop(0, wide, step, 0)
    send_mid(mid - 1)

    aa[...] = jnp.zeros_like(aa)
    bb[...] = jnp.zeros_like(bb)

    def last(h, carry):
        @pl.when(T >= 1)
        def _():
            share(0, h).wait_recv()
        pieces = []
        for k in range(3):
            pieces += thirds(m[k, h])
        total = push(0, h, l2, pieces)

        @pl.when(h >= 2)
        def _():
            out_ref[h - 2] = gate(total, q2, c2, m[0, h - 1])
        return carry

    lax.fori_loop(0, mid, last, 0)

    @pl.when(T + 2 < nt)
    def _():
        for f in range(fib):
            cross(f).wait_send()

    @pl.when(up)
    def _():
        halo_up(0, h0s, h0r).wait_send()

        @pl.when(T >= 2)
        def _():
            halo_up(2, h2s, h2r).wait_send()

    @pl.when(down)
    def _():
        halo_down(0, h0s, h0r).wait_send()

        @pl.when(T >= 2)
        def _():
            halo_down(2, h2s, h2r).wait_send()

    def drain(g, carry):
        @pl.when(even | (T >= 2))
        def _():
            part(0, g).wait_send()

        @pl.when(even & (T >= 2))
        def _():
            part3(g).wait_send()
        return carry

    lax.fori_loop(0, wide, drain, 0)

    @pl.when(even | (T >= 2))
    def _():
        for h in range(mid):
            share(0, h).wait_send()

    if far:
        for i, e, ok, _ok in thirds_list:
            @pl.when(send3 if ok is None else send3 & ok)
            def _(i=i, e=e):
                third(i, e).wait_send()


def solution(mesh):
    nt, nf = mesh.shape["tm"], mesh.shape["fibre"]
    placed = (P(None, "fibre", "tm"), P(), P(), P(), P(), P(), P())

    def body(signal, w1, b1, r1, w2, b2, r2):
        ch, fib, length = signal.shape
        assert length == DILATION_TWO == 2 * DILATION_ONE and nt % 2 == 0 and fib >= 4
        x = jnp.transpose(signal, (1, 0, 2))
        out_ch = w1.shape[2]
        b1 = b1.reshape(1, out_ch)
        b2 = b2.reshape(1, out_ch)
        dma = lambda n: pltpu.SemaphoreType.DMA((n,))
        out = pl.pallas_call(
            lambda *refs: kernel(nt, nf, fib, *refs),
            name="gated_layers",
            out_shape=jax.ShapeDtypeStruct((fib, ch, length), F32),
            in_specs=[pl.BlockSpec(memory_space=pl.ANY)] * 7,
            out_specs=pl.BlockSpec(memory_space=pltpu.VMEM),
            scratch_shapes=[
                pltpu.VMEM((4, fib + 4, ch, length), F32),
                pltpu.VMEM((3, fib + 2, ch, length), F32),
                pltpu.VMEM(w1.shape, F32), pltpu.VMEM(b1.shape, F32), pltpu.VMEM(r1.shape, F32),
                pltpu.VMEM(w2.shape, F32), pltpu.VMEM(b2.shape, F32), pltpu.VMEM(r2.shape, F32),
                pltpu.VMEM((3 * out_ch, 9 * ch), BF), pltpu.VMEM((3 * out_ch, 9 * ch), BF),
                pltpu.VMEM((ch, 3 * ch), BF), pltpu.VMEM((ch, 3 * ch), BF),
                pltpu.VMEM((out_ch, out_ch), F32), pltpu.VMEM((out_ch, out_ch), F32),
                pltpu.VMEM((2, out_ch, length), F32), pltpu.VMEM((2, out_ch, length), F32),
                dma(fib), dma(6), dma(2), dma(2), dma(fib), dma(fib), dma(2), dma(2),
                dma(fib + 4), dma(fib + 4), dma(fib + 4), dma(fib + 4),
                dma(fib + 2), dma(fib + 2), dma(3), dma(3),
            ],
            compiler_params=pltpu.CompilerParams(collective_id=0, has_side_effects=True),
        )(x, w1, b1, r1, w2, b2, r2)
        return jnp.transpose(out, (1, 0, 2))

    return jax.shard_map(body, mesh=mesh, in_specs=placed, out_specs=P(None, "fibre", "tm"), check_vma=False)
```

time: 69.6 us -> 50.2 us (0.72)
  the two profiles are of different devices: /device:TPU:0 before, /device:TPU:23 now
where the time goes in v1:
time: 50.2 us; the launch traced here: 49.9 us
  Pallas kernels  43.6 us (87%)
  local copies, waits for them, and re-layouts  6.3 us (13%)
    pallas_call x1, Pallas kernels, body(): pl.pallas_call(lambda *refs: kernel(nt, nf, fib, *refs), name='gated_laye...  43.6 us
    unnamed x7, local copies, waits for them, and re-layouts  4.15 us
    transpose x1, local copies, waits for them, and re-layouts, body(): return jnp.transpose(out, (1, 0, 2))  2.14 us

profile of v1, /device:TPU:23, one launch (start us, length us, event | category | flops | bytes accessed | tf_op | source)
XLA Modules:
  0.0 49.9 jit_solution(5839237965075811438)
XLA Ops:
  0.0 0.0 copy-start
  0.0 2.0 %copy.13 = f32[64,8,256]{2,0,1:T(8,128)} copy(f32[64,8,256]{2,1,0:T(8,128)} %param.7) | data formatting | bytes 1048576 | tf_op args[0]
  2.1 0.0 copy-done
  2.1 0.0 copy-start.1
  2.1 1.0 %copy.9.refs_1_ = f32[3,3,128,64]{3,2,1,0:T(8,128)} copy(f32[3,3,128,64]{2,3,1,0:T(8,128)S(1)} %copy-done) | data formatting | bytes 589824 | tf_op args[1]
  3.1 0.0 copy-done.1
  3.1 1.0 %copy.10.refs_4_ = f32[3,3,128,64]{3,2,1,0:T(8,128)} copy(f32[3,3,128,64]{2,3,1,0:T(8,128)S(1)} %copy-done.1) | data formatting | bytes 589824 | tf_op args[4]
  4.2 43.6 %gated_layers.1 = f32[8,64,256]{2,1,0:T(8,128)} custom-call(f32[8,64,256]{2,1,0:T(8,128)} %bitcast.7, f32[3,3,128,64]{3,2,1,0:T(8,128)} %copy.9.refs_1_, f32[1,128]{1,0:T(1,128)} %bitcast.8, f32[64,64]{1,0:T(8,128)} %refs_3_.1, f32[3,3,128,64]{3,2,1,0:T(8,128)} %copy.10.refs_4_, f32[1,128]{1,0:T(1,128)} %bitcast.9, f32[64,64]{1,0:T(8,128)} %refs_6_.1), custom_call_target="tpu_custom_call" | custom-call | tf_op jit(solution)/shard_map/gated_layers/pallas_call | solution.py:380
  47.8 2.1 %copy.11 = f32[64,8,256]{2,1,0:T(8,128)} copy(f32[64,8,256]{2,0,1:T(8,128)} %bitcast.6) | data formatting | bytes 1048576 | tf_op jit(solution)/shard_map/transpose | solution.py:401
Async XLA Ops:
  0.0 2.1 %copy-start = (f32[3,3,128,64]{2,3,1,0:T(8,128)S(1)}, f32[3,3,128,64]{2,3,1,0:T(8,128)}, u32[]{:S(2)}) copy-start(f32[3,3,128,64]{2,3,1,0:T(8,128)} %param.8) | copy-start | bytes 884740
  2.1 1.1 %copy-start.1 = (f32[3,3,128,64]{2,3,1,0:T(8,128)S(1)}, f32[3,3,128,64]{2,3,1,0:T(8,128)}, u32[]{:S(2)}) copy-start(f32[3,3,128,64]{2,3,1,0:T(8,128)} %param.11) | copy-start | bytes 884740

commit v2 on v1

v2 whole, which is shorter than its diff:
```python
import jax
import jax.numpy as jnp
from jax import lax
from jax.experimental import pallas as pl
from jax.experimental.pallas import tpu as pltpu
from jax.sharding import PartitionSpec as P

DILATION_ONE = 128
DILATION_TWO = 256
BF = jnp.bfloat16
F32 = jnp.float32


def split(value):
    hi = value.astype(BF)
    return hi, (value - hi.astype(F32)).astype(BF)


def thirds(value):
    hi, lo = split(value)
    return [hi, lo, hi]


def pick(i, values):
    out = jnp.int32(values[-1])
    for n in range(len(values) - 2, -1, -1):
        out = jnp.where(i == n, jnp.int32(values[n]), out)
    return out


def kernel(
    nt, nf, fib,
    x_hbm, w1_hbm, b1_hbm, r1_hbm, w2_hbm, b2_hbm, r2_hbm, out_ref,
    s, m, xv, w1, b1, r1, w2, b2, r2, l1, l2, q1, q2, c1, c2, acc, acc2,
    in_sem, w_sem, h0s, h0r, xs, xr, h2s, h2r, ps, pr, ts, tr, ms, mr, es, er,
):
    T = lax.axis_index("tm")
    F = lax.axis_index("fibre")
    odd = lax.rem(T, 2)
    even = odd == 0
    isodd = odd == 1
    late = T >= 2
    partner = T + 1 - 2 * odd
    ch, length = s.shape[2], s.shape[3] // 2
    own = fib // 2
    wide = own + 2
    mid = own + 1
    out_ch = 2 * ch
    far = nt > 4
    up, down = F + 1 < nf, F > 0
    arrive = [own] + list(range(1, own))
    order = [own, 0, 1, own + 1] + list(range(2, own))
    emits = [0, 0, 0, own] + list(range(1, own - 1))
    order2 = [0, own] + list(range(1, own))

    def dev(t, f):
        return {"tm": t, "fibre": f}

    load = pltpu.make_async_copy(x_hbm, xv, in_sem.at[0])
    load.start()
    weights = [
        pltpu.make_async_copy(a, b, w_sem.at[i])
        for i, (a, b) in enumerate(
            [(w1_hbm, w1), (b1_hbm, b1), (r1_hbm, r1), (w2_hbm, w2), (b2_hbm, b2), (r2_hbm, r2)]
        )
    ]
    for c in weights:
        c.start()

    barrier = pltpu.get_barrier_semaphore()
    friends = [(partner, F, None), (T, F + 1, up), (T, F - 1, down), (T + 2, F, T + 2 < nt), (T - 2, F, late)]
    if far:
        send3 = isodd & (T + 3 < nt)
        recv3 = even & (T >= 4)
        for e, ok in ((0, None), (1, up), (-1, down)):
            for d, okt in ((3, send3), (-3, recv3)):
                friends.append((T + d, F + e, okt if ok is None else okt & ok))
    count = jnp.int32(0)
    for t, f, ok in friends:
        if ok is None:
            pl.semaphore_signal(barrier, inc=1, device_id=dev(t, f), device_id_type=pl.DeviceIdType.MESH)
            count = count + 1
        else:
            @pl.when(ok)
            def _(t=t, f=f):
                pl.semaphore_signal(barrier, inc=1, device_id=dev(t, f), device_id_type=pl.DeviceIdType.MESH)
            count = count + ok.astype(jnp.int32)

    load.wait()
    for f in range(fib):
        for c in range(0, length, 128):
            s[0, 1 + f // 2, :, pl.ds((f % 2) * length + c, 128)] = xv[pl.ds(c // 128 * fib + f, ch, stride=fib * length // 128), :]
    pl.semaphore_wait(barrier, count)

    def remote(src, dst, ssem, rsem, t, f):
        return pltpu.make_async_remote_copy(
            src_ref=src, dst_ref=dst, send_sem=ssem, recv_sem=rsem,
            device_id=dev(t, f), device_id_type=pl.DeviceIdType.MESH,
        )

    def halo_up(j, ss, rr):
        return remote(s.at[j, own], s.at[j, 0], ss.at[0], rr.at[0], T, F + 1)

    def halo_down(j, ss, rr):
        return remote(s.at[j, 1], s.at[j, own + 1], ss.at[1], rr.at[1], T, F - 1)

    def cross(q):
        return remote(s.at[0, q], s.at[2, q], xs.at[q], xr.at[q], T + 2, F)

    @pl.when(T + 2 < nt)
    def _():
        for q in arrive:
            cross(q).start()

    @pl.when(up)
    def _():
        halo_up(0, h0s, h0r).start()

    @pl.when(down)
    def _():
        halo_down(0, h0s, h0r).start()

    def part(src, q):
        return remote(s.at[src, q], s.at[1, q], ps.at[q], pr.at[q], partner, F)

    def part3(q):
        return remote(s.at[2, q], s.at[3, q], ts.at[q], tr.at[q], partner, F)

    def share(src, r):
        return remote(m.at[src, r], m.at[1, r], ms.at[r], mr.at[r], partner, F)

    @pl.when(even)
    def _():
        for q in range(1, own + 1):
            part(0, q).start()

    if far:
        def third(i, e):
            if e == 0:
                src, dst = s.at[0, pl.ds(1, own)], s.at[3, pl.ds(1, own)]
            elif e == 1:
                src, dst = s.at[0, own], s.at[3, 0]
            else:
                src, dst = s.at[0, 1], s.at[3, own + 1]
            return remote(src, dst, es.at[i], er.at[i], T + 3, F + e)

        thirds_list = [(0, 0, None, None), (1, 1, up, down), (2, -1, down, up)]
        for i, e, ok, _ok in thirds_list:
            @pl.when(send3 if ok is None else send3 & ok)
            def _(i=i, e=e):
                third(i, e).start()

    zero = jnp.zeros(s.shape[2:], F32)

    def zero_halo(j):
        @pl.when(jnp.logical_not(down))
        def _():
            s[j, 0] = zero

        @pl.when(jnp.logical_not(up))
        def _():
            s[j, own + 1] = zero

    zero_halo(0)

    @pl.when(late)
    def _():
        zero_halo(2)

    @pl.when(T == 0)
    def _():
        s[1] = jnp.zeros(s.shape[1:], F32)
        m[1] = jnp.zeros(m.shape[1:], F32)

    @pl.when(T < 2)
    def _():
        m[2] = jnp.zeros(m.shape[1:], F32)

    @pl.when(T == 2)
    def _():
        s[3] = jnp.zeros(s.shape[1:], F32)

    if far:
        @pl.when(recv3)
        def _():
            zero_halo(3)

    for c in weights:
        c.wait()

    def prepare(w, left, r, mix, bias, tall):
        for a in range(3):
            for k in range(3):
                hi, lo = split(w[a, k].T)
                for i, piece in enumerate((hi, hi, lo)):
                    left[pl.ds(a * out_ch, out_ch), pl.ds((3 * k + i) * ch, ch)] = piece
        hi, lo = split(r[...])
        for i, piece in enumerate((hi, hi, lo)):
            mix[:, pl.ds(i * ch, ch)] = piece
        tall[...] = jnp.broadcast_to(bias[...], (out_ch, out_ch)).T

    prepare(w1, l1, r1, q1, b1, c1)
    acc[...] = jnp.zeros_like(acc)
    acc2[...] = jnp.zeros_like(acc2)

    @pl.when(down)
    def _():
        halo_up(0, h0s, h0r).wait_recv()

    @pl.when(up)
    def _():
        halo_down(0, h0s, h0r).wait_recv()

    @pl.when(even)
    def _():
        part(0, 0).start()
        part(0, own + 1).start()

    prepare(w2, l2, r2, q2, b2, c2)

    def push(low, high, left, pieces):
        p = jnp.dot(left[...], jnp.concatenate(pieces, axis=0), preferred_element_type=F32)
        p0, p1, p2 = p[:out_ch], p[out_ch:2 * out_ch], p[2 * out_ch:]
        n = length
        low[...] = low[...] + jnp.concatenate([p0[:, :n] + p1[:, n:], p0[:, n:]], axis=1)
        high[...] = high[...] + jnp.concatenate([p2[:, :n], p1[:, :n] + p2[:, n:]], axis=1)

    def gate(total, mix, tall, base):
        bias = tall[...]
        bias = jnp.concatenate([bias] * (total.shape[1] // bias.shape[1]), axis=1)
        pre = total + bias
        g = jnp.tanh(pre[:ch]) * (0.5 * jnp.tanh(0.5 * pre[ch:]) + 0.5)
        return base + jnp.dot(mix[...], jnp.concatenate(thirds(g), axis=0), preferred_element_type=F32)

    def straddle(ref, j, r):
        return jnp.concatenate([ref[j, r, :, length:], ref[j, r + 1, :, :length]], axis=1)

    def emit(slot, cur, r, dst):
        value = gate(acc[slot, r + 1], q1, c1, straddle(s, cur, r))
        row = F * fib + 2 * r - 1
        lo = jnp.where((row >= 0) & (row < nf * fib), value[:, :length], 0.0)
        hi = jnp.where((row + 1 >= 0) & (row + 1 < nf * fib), value[:, length:], 0.0)
        m[dst, r] = jnp.concatenate([lo, hi], axis=1)

    def first(slot, i, q, cur, prev, dst):
        chi, clo = split(s[cur, q])
        phi, plo = split(s[prev, q])
        d, n = DILATION_ONE, length

        def shift(p, c):
            return jnp.concatenate([p[:, d:n], c[:, :d], p[:, n + d:], c[:, n:n + d]], axis=1)

        shi, slo = shift(phi, chi), shift(plo, clo)
        push(acc.at[slot, q + 1], acc.at[slot, q], l1, [chi, clo, chi, shi, slo, shi, phi, plo, phi])

        @pl.when(i >= 2)
        def _():
            emit(slot, cur, jnp.where(i == wide - 1, own - 2, pick(i, emits)), dst)

    def out_emit(p):
        value = gate(acc2[p + 1], q2, c2, straddle(m, 0, p))
        for e in range(2):
            for c in range(0, length, 128):
                out_ref[pl.ds(c // 128 * fib + 2 * p + e, ch, stride=fib * length // 128), :] = value[:, e * length + c:e * length + c + 128]

    def last(i):
        r = pick(i, order2)

        @pl.when(T >= 1)
        def _():
            share(0, r).wait_recv()
        pieces = []
        for k in range(3):
            pieces += thirds(m[k, r])
        push(acc2.at[r + 1], acc2.at[r], l2, pieces)

        @pl.when(i >= 2)
        def _():
            out_emit(i - 2)

    def send_mid(r):
        @pl.when(even)
        def _():
            share(0, r).start()

        @pl.when(isodd & late)
        def _():
            share(2, r).start()

    def forward(q):
        @pl.when(even)
        def _():
            part3(q).start()

        @pl.when(isodd)
        def _():
            part(2, q).start()

    def service_top():
        cross(own).wait_recv()

        @pl.when(up)
        def _():
            halo_up(2, h2s, h2r).start()
        forward(own)

    def early(i, carry):
        q = pick(i, order)

        @pl.when(T >= 1)
        def _():
            part(0, q).wait_recv()

        @pl.when((T == 0) & (i >= 3))
        def _():
            send_mid(pick(i - 1, emits))
        first(0, i, q, 0, 1, 0)

        @pl.when(late & (i == 3))
        def _():
            service_top()
        return carry

    @pl.when(isodd | (T == 0))
    def _():
        lax.fori_loop(0, wide, early, 0)
        emit(0, 0, own - 1, 0)

        @pl.when(T == 0)
        def _():
            send_mid(own - 2)
            send_mid(own - 1)

    def stream(i, carry):
        q = pick(i, order)

        @pl.when(i >= 3)
        def _():
            send_mid(pick(i - 1, emits))

        @pl.when(i >= 4)
        def _():
            last(i - 4)

        @pl.when(even & (i == 0))
        def _():
            service_top()

        @pl.when(i == 1)
        def _():
            @pl.when(down)
            def _():
                halo_up(2, h2s, h2r).wait_recv()
            forward(q)

        @pl.when(i == 3)
        def _():
            @pl.when(up)
            def _():
                halo_down(2, h2s, h2r).wait_recv()
            forward(q)

        @pl.when((i == 2) | (i >= 4))
        def _():
            cross(q).wait_recv()

            @pl.when((i == 2) & down)
            def _():
                halo_down(2, h2s, h2r).start()
            forward(q)

        @pl.when(isodd)
        def _():
            part3(q).wait_recv()
        first(1, i, q, 2, 3, 2)

        @pl.when(even)
        def _():
            part(0, q).wait_recv()
            first(0, i, q, 0, 1, 0)
        return carry

    @pl.when(late)
    def _():
        if far:
            for i, e, _ok, ok in thirds_list:
                @pl.when(recv3 if ok is None else recv3 & ok)
                def _(i=i, e=e):
                    third(i, e).wait_recv()
        lax.fori_loop(0, wide, stream, 0)

        @pl.when(even)
        def _():
            emit(0, 0, own - 1, 0)
        emit(1, 2, own - 1, 2)
        send_mid(own - 2)
        send_mid(own - 1)

    def final(i, carry):
        last(i)
        return carry

    lax.fori_loop(jnp.where(late, wide - 4, 0), mid, final, 0)
    out_emit(own - 1)

    @pl.when(T + 2 < nt)
    def _():
        for q in arrive:
            cross(q).wait_send()

    @pl.when(up)
    def _():
        halo_up(0, h0s, h0r).wait_send()

        @pl.when(late)
        def _():
            halo_up(2, h2s, h2r).wait_send()

    @pl.when(down)
    def _():
        halo_down(0, h0s, h0r).wait_send()

        @pl.when(late)
        def _():
            halo_down(2, h2s, h2r).wait_send()

    for q in range(wide):
        @pl.when(even | late)
        def _(q=q):
            part(0, q).wait_send()

        @pl.when(even & late)
        def _(q=q):
            part3(q).wait_send()

    @pl.when(even | late)
    def _():
        for r in range(mid):
            share(0, r).wait_send()

    if far:
        for i, e, ok, _ok in thirds_list:
            @pl.when(send3 if ok is None else send3 & ok)
            def _(i=i, e=e):
                third(i, e).wait_send()


def solution(mesh):
    nt, nf = mesh.shape["tm"], mesh.shape["fibre"]
    placed = (P(None, "fibre", "tm"), P(), P(), P(), P(), P(), P())

    def body(signal, w1, b1, r1, w2, b2, r2):
        ch, fib, length = signal.shape
        assert length == DILATION_TWO == 2 * DILATION_ONE and nt % 2 == 0 and fib % 2 == 0 and fib >= 8
        x = signal.reshape(ch, fib, length // 128, 128).transpose(0, 2, 1, 3).reshape(-1, 128)
        out_ch = w1.shape[2]
        own = fib // 2
        w1, w2 = jnp.transpose(w1, (0, 1, 3, 2)), jnp.transpose(w2, (0, 1, 3, 2))
        b1 = b1.reshape(1, out_ch)
        b2 = b2.reshape(1, out_ch)
        dma = lambda n: pltpu.SemaphoreType.DMA((n,))
        out = pl.pallas_call(
            lambda *refs: kernel(nt, nf, fib, *refs),
            name="gated_layers",
            out_shape=jax.ShapeDtypeStruct(x.shape, F32),
            in_specs=[pl.BlockSpec(memory_space=pl.ANY)] * 7,
            out_specs=pl.BlockSpec(memory_space=pltpu.VMEM),
            scratch_shapes=[
                pltpu.VMEM((4, own + 2, ch, 2 * length), F32),
                pltpu.VMEM((3, own + 1, ch, 2 * length), F32),
                pltpu.VMEM(x.shape, F32),
                pltpu.VMEM(w1.shape, F32), pltpu.VMEM(b1.shape, F32), pltpu.VMEM(r1.shape, F32),
                pltpu.VMEM(w2.shape, F32), pltpu.VMEM(b2.shape, F32), pltpu.VMEM(r2.shape, F32),
                pltpu.VMEM((3 * out_ch, 9 * ch), BF), pltpu.VMEM((3 * out_ch, 9 * ch), BF),
                pltpu.VMEM((ch, 3 * ch), BF), pltpu.VMEM((ch, 3 * ch), BF),
                pltpu.VMEM((out_ch, out_ch), F32), pltpu.VMEM((out_ch, out_ch), F32),
                pltpu.VMEM((2, own + 3, out_ch, 2 * length), F32),
                pltpu.VMEM((own + 2, out_ch, 2 * length), F32),
                dma(1), dma(6), dma(2), dma(2), dma(own + 1), dma(own + 1), dma(2), dma(2),
                dma(own + 2), dma(own + 2), dma(own + 2), dma(own + 2),
                dma(own + 1), dma(own + 1), dma(3), dma(3),
            ],
            compiler_params=pltpu.CompilerParams(collective_id=0, has_side_effects=True),
        )(x, w1, b1, r1, w2, b2, r2)
        out = out.reshape(ch, length // 128, fib, 128).transpose(0, 2, 1, 3)
        return out.reshape(ch, fib, length)

    return jax.shard_map(body, mesh=mesh, in_specs=placed, out_specs=P(None, "fibre", "tm"), check_vma=False)
```

time: 50.2 us -> 33.7 us (0.67)
  Pallas kernels: 43.6 us -> 31.7 us
  local copies, waits for them, and re-layouts: 6.3 us -> 1.87 us
    pallas_call x1, Pallas kernels: 43.6 us -> 31.7 us  [body(): pl.pallas_call(lambda *refs: kernel(nt, nf, fib, *refs), name='gated_laye...]
    unnamed x7 -> x1, local copies, waits for them, and re-layouts: 4.15 us -> 1.87 us
    transpose x1 -> x0, local copies, waits for them, and re-layouts: 2.14 us -> none  [body(): return jnp.transpose(out, (1, 0, 2))]
where the time goes in v2:
time: 33.7 us; the launch traced here: 33.5 us
  Pallas kernels  31.7 us (94%)
  local copies, waits for them, and re-layouts  1.87 us (6%)
    pallas_call x1, Pallas kernels, body(): pl.pallas_call(lambda *refs: kernel(nt, nf, fib, *refs), name='gated_laye...  31.7 us
    unnamed x1, local copies, waits for them, and re-layouts  1.87 us

profile of v2, /device:TPU:23, one launch (start us, length us, event | category | flops | bytes accessed | tf_op | source)
XLA Modules:
  0.0 33.5 jit_solution(7200189363165479482)
XLA Ops:
  0.0 31.7 %gated_layers.1 = f32[1024,128]{1,0:T(8,128)} custom-call(f32[1024,128]{1,0:T(8,128)} %bitcast.15, f32[3,3,64,128]{3,2,1,0:T(8,128)} %bitcast.16, f32[1,128]{1,0:T(1,128)} %bitcast.18, f32[64,64]{1,0:T(8,128)} %refs_3_.1, f32[3,3,64,128]{3,2,1,0:T(8,128)} %bitcast.17, f32[1,128]{1,0:T(1,128)} %bitcast.19, f32[64,64]{1,0:T(8,128)} %refs_6_.1), custom_call_target="tpu_custom_call" | custom-call | tf_op jit(solution)/shard_map/gated_layers/pallas_call | solution.py:462
  31.7 1.9 %copy.9 = f32[64,8,256]{2,1,0:T(8,128)} copy(f32[64,8,256]{2,1,0:T(8,128)} %bitcast.14) | data formatting | bytes 1048576

commit v3 on v2

--- a/solution.py
+++ b/solution.py
@@ -49,9 +49,7 @@
     far = nt > 4
     up, down = F + 1 < nf, F > 0
     arrive = [own] + list(range(1, own))
-    order = [own, 0, 1, own + 1] + list(range(2, own))
-    emits = [0, 0, 0, own] + list(range(1, own - 1))
-    order2 = [0, own] + list(range(1, own))
+    order = [own] + list(range(own)) + [own + 1]
 
     def dev(t, f):
         return {"tm": t, "fibre": f}
@@ -107,18 +105,18 @@
     def cross(q):
         return remote(s.at[0, q], s.at[2, q], xs.at[q], xr.at[q], T + 2, F)
 
+    @pl.when(up)
+    def _():
+        halo_up(0, h0s, h0r).start()
+
+    @pl.when(down)
+    def _():
+        halo_down(0, h0s, h0r).start()
+
     @pl.when(T + 2 < nt)
     def _():
         for q in arrive:
             cross(q).start()
-
-    @pl.when(up)
-    def _():
-        halo_up(0, h0s, h0r).start()
-
-    @pl.when(down)
-    def _():
-        halo_down(0, h0s, h0r).start()
 
     def part(src, q):
         return remote(s.at[src, q], s.at[1, q], ps.at[q], pr.at[q], partner, F)
@@ -163,9 +161,9 @@
 
     zero_halo(0)
 
-    @pl.when(late)
-    def _():
-        zero_halo(2)
+    @pl.when(late & jnp.logical_not(down))
+    def _():
+        s[2, 0] = zero
 
     @pl.when(T == 0)
     def _():
@@ -211,6 +209,10 @@
     def _():
         halo_down(0, h0s, h0r).wait_recv()
 
+    @pl.when(T + 2 < nt)
+    def _():
+        cross(own + 1).start()
+
     @pl.when(even)
     def _():
         part(0, 0).start()
@@ -255,7 +257,7 @@
 
         @pl.when(i >= 2)
         def _():
-            emit(slot, cur, jnp.where(i == wide - 1, own - 2, pick(i, emits)), dst)
+            emit(slot, cur, jnp.where(i == wide - 1, own, i - 2), dst)
 
     def out_emit(p):
         value = gate(acc2[p + 1], q2, c2, straddle(m, 0, p))
@@ -264,7 +266,7 @@
                 out_ref[pl.ds(c // 128 * fib + 2 * p + e, ch, stride=fib * length // 128), :] = value[:, e * length + c:e * length + c + 128]
 
     def last(i):
-        r = pick(i, order2)
+        r = i
 
         @pl.when(T >= 1)
         def _():
@@ -274,9 +276,9 @@
             pieces += thirds(m[k, r])
         push(acc2.at[r + 1], acc2.at[r], l2, pieces)
 
-        @pl.when(i >= 2)
-        def _():
-            out_emit(i - 2)
+        @pl.when(i >= 1)
+        def _():
+            out_emit(i - 1)
 
     def send_mid(r):
         @pl.when(even)
@@ -313,7 +315,7 @@
 
         @pl.when((T == 0) & (i >= 3))
         def _():
-            send_mid(pick(i - 1, emits))
+            send_mid(i - 3)
         first(0, i, q, 0, 1, 0)
 
         @pl.when(late & (i == 3))
@@ -328,7 +330,7 @@
 
         @pl.when(T == 0)
         def _():
-            send_mid(own - 2)
+            send_mid(own)
             send_mid(own - 1)
 
     def stream(i, carry):
@@ -336,7 +338,7 @@
 
         @pl.when(i >= 3)
         def _():
-            send_mid(pick(i - 1, emits))
+            send_mid(i - 3)
 
         @pl.when(i >= 4)
         def _():
@@ -353,20 +355,9 @@
                 halo_up(2, h2s, h2r).wait_recv()
             forward(q)
 
-        @pl.when(i == 3)
-        def _():
-            @pl.when(up)
-            def _():
-                halo_down(2, h2s, h2r).wait_recv()
-            forward(q)
-
-        @pl.when((i == 2) | (i >= 4))
+        @pl.when(i >= 2)
         def _():
             cross(q).wait_recv()
-
-            @pl.when((i == 2) & down)
-            def _():
-                halo_down(2, h2s, h2r).start()
             forward(q)
 
         @pl.when(isodd)
@@ -393,7 +384,7 @@
         def _():
             emit(0, 0, own - 1, 0)
         emit(1, 2, own - 1, 2)
-        send_mid(own - 2)
+        send_mid(own)
         send_mid(own - 1)
 
     def final(i, carry):
@@ -401,11 +392,9 @@
         return carry
 
     lax.fori_loop(jnp.where(late, wide - 4, 0), mid, final, 0)
-    out_emit(own - 1)
-
     @pl.when(T + 2 < nt)
     def _():
-        for q in arrive:
+        for q in arrive + [own + 1]:
             cross(q).wait_send()
 
     @pl.when(up)
@@ -419,10 +408,6 @@
     @pl.when(down)
     def _():
         halo_down(0, h0s, h0r).wait_send()
-
-        @pl.when(late)
-        def _():
-            halo_down(2, h2s, h2r).wait_send()
 
     for q in range(wide):
         @pl.when(even | late)
@@ -476,7 +461,7 @@
                 pltpu.VMEM((out_ch, out_ch), F32), pltpu.VMEM((out_ch, out_ch), F32),
                 pltpu.VMEM((2, own + 3, out_ch, 2 * length), F32),
                 pltpu.VMEM((own + 2, out_ch, 2 * length), F32),
-                dma(1), dma(6), dma(2), dma(2), dma(own + 1), dma(own + 1), dma(2), dma(2),
+                dma(1), dma(6), dma(2), dma(2), dma(own + 2), dma(own + 2), dma(2), dma(2),
                 dma(own + 2), dma(own + 2), dma(own + 2), dma(own + 2),
                 dma(own + 1), dma(own + 1), dma(3), dma(3),
             ],

time: 33.7 us -> 32 us (0.950)
  Pallas kernels: 31.7 us -> 29.9 us
    pallas_call x1, Pallas kernels: 31.7 us -> 29.9 us  [body(): pl.pallas_call(lambda *refs: kernel(nt, nf, fib, *refs), name='gated_laye...]
where the time goes in v3:
time: 32 us; the launch traced here: 31.8 us
  Pallas kernels  29.9 us (93%)
  local copies, waits for them, and re-layouts  1.87 us (6%)
    pallas_call x1, Pallas kernels, body(): pl.pallas_call(lambda *refs: kernel(nt, nf, fib, *refs), name='gated_laye...  29.9 us
    unnamed x1, local copies, waits for them, and re-layouts  1.87 us

profile of v3, /device:TPU:23, one launch (start us, length us, event | category | flops | bytes accessed | tf_op | source)
XLA Modules:
  0.0 31.8 jit_solution(3247611589328736428)
XLA Ops:
  0.0 29.9 %gated_layers.1 = f32[1024,128]{1,0:T(8,128)} custom-call(f32[1024,128]{1,0:T(8,128)} %bitcast.15, f32[3,3,64,128]{3,2,1,0:T(8,128)} %bitcast.16, f32[1,128]{1,0:T(1,128)} %bitcast.18, f32[64,64]{1,0:T(8,128)} %refs_3_.1, f32[3,3,64,128]{3,2,1,0:T(8,128)} %bitcast.17, f32[1,128]{1,0:T(1,128)} %bitcast.19, f32[64,64]{1,0:T(8,128)} %refs_6_.1), custom_call_target="tpu_custom_call" | custom-call | tf_op jit(solution)/shard_map/gated_layers/pallas_call | solution.py:447
  29.9 1.9 %copy.9 = f32[64,8,256]{2,1,0:T(8,128)} copy(f32[64,8,256]{2,1,0:T(8,128)} %bitcast.14) | data formatting | bytes 1048576

commit v4 on v3

--- a/solution.py
+++ b/solution.py
@@ -32,7 +32,7 @@
     nt, nf, fib,
     x_hbm, w1_hbm, b1_hbm, r1_hbm, w2_hbm, b2_hbm, r2_hbm, out_ref,
     s, m, xv, w1, b1, r1, w2, b2, r2, l1, l2, q1, q2, c1, c2, acc, acc2,
-    in_sem, w_sem, h0s, h0r, xs, xr, h2s, h2r, ps, pr, ts, tr, ms, mr, es, er,
+    in_sem, w_sem, h0s, h0r, xs, xr, ps, pr, ts, tr, ms, mr, es, er,
 ):
     T = lax.axis_index("tm")
     F = lax.axis_index("fibre")
@@ -48,8 +48,9 @@
     out_ch = 2 * ch
     far = nt > 4
     up, down = F + 1 < nf, F > 0
-    arrive = [own] + list(range(1, own))
-    order = [own] + list(range(own)) + [own + 1]
+    arrive = list(range(1, own + 1))
+    order = arrive + [0, own + 1]
+    order2 = list(range(1, own)) + [0, own]
 
     def dev(t, f):
         return {"tm": t, "fibre": f}
@@ -161,9 +162,6 @@
 
     zero_halo(0)
 
-    @pl.when(late & jnp.logical_not(down))
-    def _():
-        s[2, 0] = zero
 
     @pl.when(T == 0)
     def _():
@@ -211,6 +209,7 @@
 
     @pl.when(T + 2 < nt)
     def _():
+        cross(0).start()
         cross(own + 1).start()
 
     @pl.when(even)
@@ -237,6 +236,9 @@
     def straddle(ref, j, r):
         return jnp.concatenate([ref[j, r, :, length:], ref[j, r + 1, :, :length]], axis=1)
 
+    def ready(i):
+        return jnp.where(i < own, i, jnp.where(i == own, 0, own))
+
     def emit(slot, cur, r, dst):
         value = gate(acc[slot, r + 1], q1, c1, straddle(s, cur, r))
         row = F * fib + 2 * r - 1
@@ -255,9 +257,9 @@
         shi, slo = shift(phi, chi), shift(plo, clo)
         push(acc.at[slot, q + 1], acc.at[slot, q], l1, [chi, clo, chi, shi, slo, shi, phi, plo, phi])
 
-        @pl.when(i >= 2)
-        def _():
-            emit(slot, cur, jnp.where(i == wide - 1, own, i - 2), dst)
+        @pl.when(i >= 1)
+        def _():
+            emit(slot, cur, ready(i), dst)
 
     def out_emit(p):
         value = gate(acc2[p + 1], q2, c2, straddle(m, 0, p))
@@ -266,7 +268,7 @@
                 out_ref[pl.ds(c // 128 * fib + 2 * p + e, ch, stride=fib * length // 128), :] = value[:, e * length + c:e * length + c + 128]
 
     def last(i):
-        r = i
+        r = pick(i, order2)
 
         @pl.when(T >= 1)
         def _():
@@ -278,7 +280,7 @@
 
         @pl.when(i >= 1)
         def _():
-            out_emit(i - 1)
+            out_emit(jnp.where(i < own - 1, i, jnp.where(i == own - 1, 0, own - 1)))
 
     def send_mid(r):
         @pl.when(even)
@@ -298,14 +300,6 @@
         def _():
             part(2, q).start()
 
-    def service_top():
-        cross(own).wait_recv()
-
-        @pl.when(up)
-        def _():
-            halo_up(2, h2s, h2r).start()
-        forward(own)
-
     def early(i, carry):
         q = pick(i, order)
 
@@ -313,52 +307,34 @@
         def _():
             part(0, q).wait_recv()
 
-        @pl.when((T == 0) & (i >= 3))
-        def _():
-            send_mid(i - 3)
+        @pl.when((T == 0) & (i >= 2))
+        def _():
+            send_mid(ready(i - 1))
         first(0, i, q, 0, 1, 0)
 
-        @pl.when(late & (i == 3))
-        def _():
-            service_top()
         return carry
 
     @pl.when(isodd | (T == 0))
     def _():
         lax.fori_loop(0, wide, early, 0)
-        emit(0, 0, own - 1, 0)
 
         @pl.when(T == 0)
         def _():
             send_mid(own)
-            send_mid(own - 1)
 
     def stream(i, carry):
         q = pick(i, order)
 
+        @pl.when(i >= 2)
+        def _():
+            send_mid(ready(i - 1))
+
         @pl.when(i >= 3)
         def _():
-            send_mid(i - 3)
-
-        @pl.when(i >= 4)
-        def _():
-            last(i - 4)
-
-        @pl.when(even & (i == 0))
-        def _():
-            service_top()
-
-        @pl.when(i == 1)
-        def _():
-            @pl.when(down)
-            def _():
-                halo_up(2, h2s, h2r).wait_recv()
-            forward(q)
-
-        @pl.when(i >= 2)
-        def _():
-            cross(q).wait_recv()
-            forward(q)
+            last(i - 3)
+
+        cross(q).wait_recv()
+        forward(q)
 
         @pl.when(isodd)
         def _():
@@ -379,31 +355,21 @@
                 def _(i=i, e=e):
                     third(i, e).wait_recv()
         lax.fori_loop(0, wide, stream, 0)
-
-        @pl.when(even)
-        def _():
-            emit(0, 0, own - 1, 0)
-        emit(1, 2, own - 1, 2)
         send_mid(own)
-        send_mid(own - 1)
 
     def final(i, carry):
         last(i)
         return carry
 
-    lax.fori_loop(jnp.where(late, wide - 4, 0), mid, final, 0)
+    lax.fori_loop(jnp.where(late, wide - 3, 0), mid, final, 0)
     @pl.when(T + 2 < nt)
     def _():
-        for q in arrive + [own + 1]:
+        for q in order:
             cross(q).wait_send()
 
     @pl.when(up)
     def _():
         halo_up(0, h0s, h0r).wait_send()
-
-        @pl.when(late)
-        def _():
-            halo_up(2, h2s, h2r).wait_send()
 
     @pl.when(down)
     def _():
@@ -461,7 +427,7 @@
                 pltpu.VMEM((out_ch, out_ch), F32), pltpu.VMEM((out_ch, out_ch), F32),
                 pltpu.VMEM((2, own + 3, out_ch, 2 * length), F32),
                 pltpu.VMEM((own + 2, out_ch, 2 * length), F32),
-                dma(1), dma(6), dma(2), dma(2), dma(own + 2), dma(own + 2), dma(2), dma(2),
+                dma(1), dma(6), dma(2), dma(2), dma(own + 2), dma(own + 2),
                 dma(own + 2), dma(own + 2), dma(own + 2), dma(own + 2),
                 dma(own + 1), dma(own + 1), dma(3), dma(3),
             ],

time: 32 us -> 30.9 us (0.966)
  the two profiles are of different devices: /device:TPU:23 before, /device:TPU:27 now
where the time goes in v4:
time: 30.9 us; the launch traced here: 30.8 us
  Pallas kernels  28.9 us (94%)
  local copies, waits for them, and re-layouts  1.87 us (6%)
    pallas_call x1, Pallas kernels, body(): pl.pallas_call(lambda *refs: kernel(nt, nf, fib, *refs), name='gated_laye...  28.9 us
    unnamed x1, local copies, waits for them, and re-layouts  1.87 us

profile of v4, /device:TPU:27, one launch (start us, length us, event | category | flops | bytes accessed | tf_op | source)
XLA Modules:
  0.0 30.8 jit_solution(2119155060863875904)
XLA Ops:
  0.0 28.9 %gated_layers.1 = f32[1024,128]{1,0:T(8,128)} custom-call(f32[1024,128]{1,0:T(8,128)} %bitcast.15, f32[3,3,64,128]{3,2,1,0:T(8,128)} %bitcast.16, f32[1,128]{1,0:T(1,128)} %bitcast.18, f32[64,64]{1,0:T(8,128)} %refs_3_.1, f32[3,3,64,128]{3,2,1,0:T(8,128)} %bitcast.17, f32[1,128]{1,0:T(1,128)} %bitcast.19, f32[64,64]{1,0:T(8,128)} %refs_6_.1), custom_call_target="tpu_custom_call" | custom-call | tf_op jit(solution)/shard_map/gated_layers/pallas_call | solution.py:413
  28.9 1.9 %copy.9 = f32[64,8,256]{2,1,0:T(8,128)} copy(f32[64,8,256]{2,1,0:T(8,128)} %bitcast.14) | data formatting | bytes 1048576
